TPU v7x, 128 devices: a whole 4x4x4 slice. The times are simulated.
128 devices in a mesh: req: 16 (over y, x), tp: 8 (over z, core).
Axes of the slice: x: 4, y: 4, z: 4, core: 2. Of those that a mesh axis runs over, the one named last changes fastest.
Arguments:
- stream: bfloat16 [512, 2048], P('req'), may hold values from -1.5 to 1.5
- attn_gain: bfloat16 [2048], replicated, may hold values from 0.25 to 1.75
- mlp_gain: bfloat16 [2048], replicated, may hold values from 0.25 to 1.75
- w_query: bfloat16 [2048, 2048], P(None, 'tp'), may hold values from -0.125 to 0.125
- w_keyval: bfloat16 [2048, 2, 2048], P(None, None, 'tp'), may hold values from -30 to 30
- w_out: bfloat16 [2048, 2048], P('tp'), may hold values from -0.125 to 0.125
- w_gate_up: bfloat16 [2048, 2, 8192], P(None, None, 'tp'), may hold values from -0.125 to 0.125
- w_down: bfloat16 [8192, 2048], P('tp'), may hold values from -0.0625 to 0.0625
- root_cache: bfloat16 [8, 4096, 2, 2048], P(None, 'req', None, 'tp'), may hold values from -240 to 240
- mid_cache: bfloat16 [16, 2048, 2, 2048], P('req', None, None, 'tp'), may hold values from -240 to 240
- leaf_cache: bfloat16 [512, 128, 2, 2048], P('req', None, None, 'tp'), may hold values from -240 to 240
- held_hidden: bfloat16 [16, 256, 2048], P('req', None, 'tp'), may hold values from -6 to 6
- recompute_rows: int32 [16, 256], P('req'), may hold values from 0 to 2047, as said below
- root_len: int32 [8], replicated, may hold values from 1024 to 4096
- mid_len: int32 [16], replicated, may hold values from 256 to 2048
- leaf_len: int32 [512], P('req'), may hold values from 1 to 128
- mid_parent: int32 [16], replicated, may hold values from 0 to 7
- leaf_parent: int32 [512], replicated, may hold values from 0 to 15
Outputs:
- layer_out: bfloat16 [512, 2048], P('req', 'tp')
Inputs may be any that keep to these rules, and one draw needn't show every extreme that they name: `recompute_rows`: the 256 slots of one middle node are distinct.
All inputs are finite; a program needn't handle non-finite values.
Results may differ from a plain program's by a relative error of at most 0.02.
The roundings to bfloat16 on the way count: a program that leaves them out, or rounds other values in their place, can miss the bound.
Values may be sent and summed in bfloat16 or wider, within the bound.
A program may use at most 192 MiB of HBM per device.

v0:
```python
import math
import jax
import jax.numpy as jnp
from jax import lax
from jax.sharding import PartitionSpec as P

D = 2048
HEAD_DIM = 64
EPSILON = 1e-05
THETA_BASE = 130000.0
NEG_FILL = -1e30


def combined_all(value, axis, combine):
    everything = jax.tree.map(lambda part: lax.all_gather(part, axis), value)
    first = jax.tree.map(lambda part: part[0], everything)

    def lap(k, so_far):
        return combine(so_far, jax.tree.map(lambda part: part[k], everything))

    return lax.fori_loop(1, lax.axis_size(axis), lap, first)


def rms_scale(values, gain):
    return (
        values
        * lax.rsqrt(jnp.mean(values * values, axis=-1, keepdims=True) + EPSILON)
        * gain.astype(jnp.float32)
    )


def rotate(values, positions):
    half_dim = values.shape[-1] // 2
    inv_freq = jnp.exp(
        jnp.arange(half_dim, dtype=jnp.float32) * (-2.0 * math.log(THETA_BASE) / values.shape[-1])
    )
    angles = positions.astype(jnp.float32)[..., None, None] * inv_freq
    cosines = jnp.cos(angles)
    sines = jnp.sin(angles)
    leading = values[..., :half_dim]
    trailing = values[..., half_dim:]
    return jnp.concatenate(
        [leading * cosines - trailing * sines, trailing * cosines + leading * sines], axis=-1
    )


def lookup(table_values, indices):
    hits = indices[..., None] == jnp.arange(table_values.shape[0], dtype=jnp.int32)
    return jnp.sum(jnp.where(hits, table_values, 0), axis=-1)


def partial_softmax(queries, key_rows, live_mask, score_scale):
    count = key_rows.shape[0]
    heads = queries.shape[1]
    key_part = key_rows[:, 0].reshape(count, heads, HEAD_DIM)
    value_part = key_rows[:, 1].reshape(count, heads, HEAD_DIM)
    scores = (
        jnp.einsum("bhd,khd->hbk", queries, key_part, preferred_element_type=jnp.float32)
        * score_scale
    )
    live = live_mask[None]
    row_max = jnp.max(jnp.where(live, scores, NEG_FILL), axis=2)
    weights = jnp.where(live, jnp.exp(scores - row_max[..., None]), 0.0)
    row_sum = jnp.sum(weights, axis=2)
    weighted = jnp.einsum(
        "hbk,khd->bhd", weights.astype(jnp.bfloat16), value_part, preferred_element_type=jnp.float32
    )
    return (row_max.T, row_sum.T, weighted.reshape(queries.shape[0], heads * HEAD_DIM))


def join(earlier, latter):
    best = jnp.maximum(earlier[0], latter[0])
    factor_one = jnp.exp(earlier[0] - best)
    factor_two = jnp.exp(latter[0] - best)
    row_sum = earlier[1] * factor_one + latter[1] * factor_two
    weighted = earlier[2] * jnp.repeat(factor_one, HEAD_DIM, axis=1) + latter[2] * jnp.repeat(
        factor_two, HEAD_DIM, axis=1
    )
    return (best, row_sum, weighted)


def leaf_softmax(queries, leaf_cache, leaf_len, score_scale):
    own_rows, slots = leaf_cache.shape[:2]
    heads = queries.shape[1]
    key_part = leaf_cache[:, :, 0].reshape(own_rows, slots, heads, HEAD_DIM)
    value_part = leaf_cache[:, :, 1].reshape(own_rows, slots, heads, HEAD_DIM)
    scores = (
        jnp.einsum("rhd,rkhd->rhk", queries, key_part, preferred_element_type=jnp.float32)
        * score_scale
    )
    live = (jnp.arange(slots, dtype=jnp.int32)[None, :] < leaf_len[:, None])[:, None, :]
    row_max = jnp.max(jnp.where(live, scores, NEG_FILL), axis=2)
    weights = jnp.where(live, jnp.exp(scores - row_max[..., None]), 0.0)
    row_sum = jnp.sum(weights, axis=2)
    weighted = jnp.einsum(
        "rhk,rkhd->rhd",
        weights.astype(jnp.bfloat16),
        value_part,
        preferred_element_type=jnp.float32,
    )
    return (row_max, row_sum, weighted)


def on_device(
    stream,
    attn_gain,
    mlp_gain,
    w_query,
    w_keyval,
    w_out,
    w_gate_up,
    w_down,
    root_cache,
    mid_cache,
    leaf_cache,
    held_hidden,
    recompute_rows,
    root_len,
    mid_len,
    leaf_len,
    mid_parent,
    leaf_parent,
):
    req_rank = lax.axis_index("req")
    own_rows = stream.shape[0]
    query_width = w_query.shape[1]
    local_heads = query_width // HEAD_DIM
    score_scale = HEAD_DIM ** (-0.5)
    requests = leaf_parent.shape[0]
    all_roots = lookup(mid_parent, leaf_parent)
    own_mids = lax.dynamic_slice_in_dim(leaf_parent, req_rank * own_rows, own_rows)
    own_roots = lax.dynamic_slice_in_dim(all_roots, req_rank * own_rows, own_rows)
    positions = lookup(root_len, own_roots) + lookup(mid_len, own_mids) + leaf_len
    stream_float = stream.astype(jnp.float32)
    normed = rms_scale(stream_float, attn_gain).astype(jnp.bfloat16)
    keyval_flat = w_keyval.reshape(D, 2 * query_width)
    queries = rotate(
        jnp.dot(normed, w_query, preferred_element_type=jnp.float32).reshape(
            own_rows, local_heads, HEAD_DIM
        ),
        positions,
    ).astype(jnp.bfloat16)
    fresh = jnp.dot(normed, keyval_flat, preferred_element_type=jnp.float32).reshape(
        own_rows, 2, local_heads, HEAD_DIM
    )
    key_new = rotate(fresh[:, 0], positions).astype(jnp.bfloat16)
    value_new = fresh[:, 1].astype(jnp.bfloat16)
    node_count, slots = mid_cache.shape[:2]
    recomp_count = recompute_rows.shape[1]
    held = lax.all_gather(held_hidden, "tp", axis=2, tiled=True)
    held_normed = rms_scale(held.astype(jnp.float32), attn_gain).astype(jnp.bfloat16)
    rebuilt = jnp.dot(
        held_normed.reshape(node_count * recomp_count, D),
        keyval_flat,
        preferred_element_type=jnp.float32,
    ).reshape(node_count, recomp_count, 2, local_heads, HEAD_DIM)
    own_nodes = req_rank * node_count + jnp.arange(node_count, dtype=jnp.int32)
    own_lens = lax.dynamic_slice_in_dim(mid_len, req_rank * node_count, node_count)
    own_parents = lax.dynamic_slice_in_dim(mid_parent, req_rank * node_count, node_count)
    rebuilt_pos = lookup(root_len, own_parents)[:, None] + recompute_rows
    rebuilt = (
        jnp.stack([rotate(rebuilt[:, :, 0], rebuilt_pos), rebuilt[:, :, 1]], axis=2)
        .astype(jnp.bfloat16)
        .reshape(node_count * recomp_count, 2, query_width)
    )
    all_queries = lax.all_gather(
        queries.reshape(own_rows, query_width), "req", axis=0, tiled=True
    ).reshape(requests, local_heads, HEAD_DIM)
    root_count, slice_len = root_cache.shape[:2]
    token_ids = req_rank * slice_len + jnp.arange(slice_len, dtype=jnp.int32)
    root_valid = token_ids[None, :] < root_len[:, None]
    root_match = all_roots[:, None] == jnp.arange(root_count, dtype=jnp.int32)[None, :]
    root_mask = (root_match[:, :, None] & root_valid[None]).reshape(
        requests, root_count * slice_len
    )
    root_part = partial_softmax(
        all_queries,
        root_cache.reshape(root_count * slice_len, 2, query_width),
        root_mask,
        score_scale,
    )
    replaced = jnp.any(
        recompute_rows[:, :, None] == jnp.arange(slots, dtype=jnp.int32)[None, None, :], axis=1
    )
    slot_live = (jnp.arange(slots, dtype=jnp.int32)[None, :] < own_lens[:, None]) & jnp.logical_not(
        replaced
    )
    belongs = leaf_parent[:, None] == own_nodes[None, :]
    held_mask = (belongs[:, :, None] & slot_live[None]).reshape(requests, node_count * slots)
    fresh_mask = (belongs[:, :, None] & (recompute_rows < own_lens[:, None])[None]).reshape(
        requests, node_count * recomp_count
    )
    mid_keys = jnp.concatenate(
        [mid_cache.reshape(node_count * slots, 2, query_width), rebuilt], axis=0
    )
    mid_part = partial_softmax(
        all_queries, mid_keys, jnp.concatenate([held_mask, fresh_mask], axis=1), score_scale
    )
    part_max, part_sum, part_acc = join(root_part, mid_part)
    merged_max, merged_sum, merged_acc = combined_all((part_max, part_sum, part_acc), "req", join)
    remote_max = lax.dynamic_slice_in_dim(merged_max, req_rank * own_rows, own_rows, 0)[None]
    remote_sum = lax.dynamic_slice_in_dim(merged_sum, req_rank * own_rows, own_rows, 0)[None]
    remote_acc = lax.dynamic_slice_in_dim(merged_acc, req_rank * own_rows, own_rows, 0)[None]
    leaf_max, leaf_sum, leaf_acc = leaf_softmax(queries, leaf_cache, leaf_len, score_scale)
    self_score = (
        jnp.sum(queries.astype(jnp.float32) * key_new.astype(jnp.float32), axis=-1) * score_scale
    )
    best = jnp.maximum(jnp.maximum(jnp.max(remote_max, axis=0), leaf_max), self_score)
    remote_factor = jnp.exp(remote_max - best[None])
    leaf_factor = jnp.exp(leaf_max - best)
    self_factor = jnp.exp(self_score - best)
    row_sum = jnp.sum(remote_sum * remote_factor, axis=0) + leaf_sum * leaf_factor + self_factor
    sources = remote_acc.shape[0]
    weighted = jnp.sum(
        remote_acc.reshape(sources, own_rows, local_heads, HEAD_DIM) * remote_factor[..., None],
        axis=0,
    )
    weighted = (
        weighted
        + leaf_acc * leaf_factor[..., None]
        + value_new.astype(jnp.float32) * self_factor[..., None]
    )
    attended = (weighted / row_sum[..., None]).reshape(own_rows, query_width).astype(jnp.bfloat16)
    attn_part = jnp.dot(attended, w_out, preferred_element_type=jnp.float32)
    width_share = D // lax.axis_size("tp")
    tp_rank = lax.axis_index("tp")
    residual = stream_float + lax.psum(attn_part, "tp")
    mixed_in = rms_scale(residual, mlp_gain).astype(jnp.bfloat16)
    residual_share = lax.dynamic_slice_in_dim(residual, tp_rank * width_share, width_share, 1)
    hidden_width = w_gate_up.shape[2]
    projected = jnp.dot(
        mixed_in, w_gate_up.reshape(D, 2 * hidden_width), preferred_element_type=jnp.float32
    ).reshape(own_rows, 2, hidden_width)
    hidden = (jax.nn.silu(projected[:, 0]) * projected[:, 1]).astype(jnp.bfloat16)
    down_share = lax.psum_scatter(
        jnp.dot(hidden, w_down, preferred_element_type=jnp.float32),
        "tp",
        scatter_dimension=1,
        tiled=True,
    )
    return (residual_share + down_share).astype(jnp.bfloat16)


def solution(mesh):
    placed = (
        P("req", None),
        P(),
        P(),
        P(None, "tp"),
        P(None, None, "tp"),
        P("tp", None),
        P(None, None, "tp"),
        P("tp", None),
        P(None, "req", None, "tp"),
        P("req", None, None, "tp"),
        P("req", None, None, "tp"),
        P("req", None, "tp"),
        P("req", None),
        P(),
        P(),
        P("req"),
        P(),
        P(),
    )
    return jax.shard_map(
        on_device, mesh=mesh, in_specs=placed, out_specs=P("req", "tp"), check_vma=False
    )
```

profile of v0, /device:TPU:0, one launch (start us, length us, event | category | flops | bytes accessed | tf_op | source)
XLA Modules:
  0.0 369.5 jit_solution(2306715656610677094)
XLA Ops:
  9.8 1.3 dynamic_slice.57
  11.1 1.2 dynamic_slice.56
  13.7 1.0 fusion.36
  14.8 1.6 fusion.62
  16.6 2.1 copy.109
  18.7 2.5 copy.77
  21.2 2.8 fusion.44
  26.2 24.1 %all_gather.22 = bf16[512,256]{1,0:T(8,128)(2,1)S(1)} all-gather(bf16[32,256]{1,0:T(8,128)(2,1)S(1)} %convert_element_type.81), channel_id=1, replica_groups=mesh['req'=16,'tp'=8] {'req'}, dimensions={0}, use_global_device_ids=true | all-gather | bytes 278528 | tf_op jit(solution)/shard_map/all_gather | solution.py:166
  51.2 1.8 and.64
  53.0 1.6 copy.107
  54.6 4.2 %fusion.81 = (bf16[2048,1,256]{2,1,0:T(2,128)(2,1)}, bf16[2048,1,256]{2,1,0:T(2,128)(2,1)}) fusion(bf16[2048,2,256]{2,1,0:T(2,128)(2,1)S(1)} %bitcast.183), kind=kLoop, calls=%fused_computation.143 | loop fusion | bytes 4194304 | tf_op jit(solution)/shard_map/slice | solution.py:56
  58.8 6.0 %copy.103 = bf16[2048,1,256]{0,2,1:T(8,128)(2,1)} copy(bf16[2048,1,256]{2,1,0:T(2,128)(2,1)} %get-tuple-element.234) | data formatting | bytes 2097152
  64.8 1.3 fusion.70
  69.3 1.5 broadcast_and_fusion
  71.6 4.3 %copy.104 = bf16[2048,1,256]{0,2,1:T(8,128)(2,1)} copy(bf16[2048,1,256]{2,1,0:T(2,128)(2,1)S(1)} %copy-done.4) | data formatting | bytes 2097152
  75.9 1.9 broadcast_and_fusion.1
  77.9 2.5 pad_add_fusion
  80.3 4.5 %select_reduce_fusion.1 = (f32[4,512]{1,0:T(4,128)S(1)}, f32[4,512,2048]{2,1,0:T(8,128)S(1)}) fusion(pred[512,2048]{1,0:T(8,128)(4,1)S(1)} %broadcast_and_fusion.1, bf16[512,4,64]{0,2,1:T(8,128)(2,1)} %bitcast.189, bf16[2048,4,64]{0,2,1:T(8,128)(2,1)S(1)} %bitcast.188), kind=kOutput, calls=%fused_computation.13 | convolution fusion | flops 549451776 | bytes 19144704 | tf_op jit(solution)/shard_map/bhd,khd->hbk/dot_general | solution.py:58
  84.9 5.7 %copy-done.1 = f32[4,512,2048]{2,1,0:T(8,128)} copy-done((f32[4,512,2048]{2,1,0:T(8,128)}, f32[4,512,2048]{2,1,0:T(8,128)S(1)}, u32[]{:S(2)}) %copy-start.1) | copy-done | bytes 16777240
  90.6 5.2 %fusion.6 = f32[4,512]{1,0:T(4,128)} fusion(f32[4,512,2048]{2,1,0:T(8,128)S(1)} %get-tuple-element.253, f32[4,512]{1,0:T(4,128)S(1)} %get-tuple-element.252, pred[512,2048]{1,0:T(8,128)(4,1)S(1)} %broadcast_and_fusion.1), kind=kLoop, calls=%fused_computation.17 | loop fusion | flops 16775168 | bytes 17842176 | tf_op jit(solution)/shard_map/reduce_sum | solution.py:64
  95.8 1.5 fusion.13
  97.3 2.8 convolution_bitcast_fusion
  100.6 13.3 %maximum_maximum_fusion = bf16[2304,2,256]{2,1,0:T(2,128)(2,1)S(1)} fusion(bf16[256,1,256]{2,1,0:T(2,128)(2,1)S(1)} %copy.79, bf16[256,1,256]{2,1,0:T(2,128)(2,1)S(1)} %copy.78, bf16[2048,2,256]{2,1,0:T(2,128)(2,1)} %bitcast.196), kind=kLoop, calls=%fused_computation.25 | loop fusion | flops 7077888 | bytes 4718592 | tf_op jit(solution)/shard_map/concatenate | solution.py:193
  113.9 4.8 %fusion.80 = (bf16[2304,1,256]{2,1,0:T(2,128)(2,1)}, bf16[2304,1,256]{2,1,0:T(2,128)(2,1)}) fusion(bf16[2304,2,256]{2,1,0:T(2,128)(2,1)S(1)} %maximum_maximum_fusion), kind=kLoop, calls=%fused_computation.142 | loop fusion | bytes 4718592 | tf_op jit(solution)/shard_map/slice | solution.py:56
  118.7 6.0 %copy.80 = bf16[2304,1,256]{0,2,1:T(8,128)(2,1)} copy(bf16[2304,1,256]{2,1,0:T(2,128)(2,1)} %get-tuple-element.232) | data formatting | bytes 2359296 | tf_op jit(solution)/shard_map/slice | solution.py:55
  124.7 6.0 %copy.82 = bf16[2304,1,256]{0,2,1:T(8,128)(2,1)} copy(bf16[2304,1,256]{2,1,0:T(2,128)(2,1)} %get-tuple-element.231) | data formatting | bytes 2359296 | tf_op jit(solution)/shard_map/slice | solution.py:56
  130.7 5.6 %select_reduce_fusion = (f32[4,512]{1,0:T(4,128)S(1)}, f32[4,512,2304]{2,1,0:T(8,128)S(1)}) fusion(pred[512,2304]{1,0:T(8,128)(4,1)} %pad_add_fusion, bf16[512,4,64]{0,2,1:T(8,128)(2,1)} %bitcast.190, bf16[2304,4,64]{0,2,1:T(8,128)(2,1)} %bitcast.187), kind=kOutput, calls=%fused_computation.11 | convolution fusion | flops 618133504 | bytes 21504000 | tf_op jit(solution)/shard_map/bhd,khd->hbk/dot_general | solution.py:58
  136.4 5.1 %fusion.4 = f32[4,512]{1,0:T(4,128)S(1)} fusion(f32[4,512,2304]{2,1,0:T(8,128)S(1)} %get-tuple-element.251, f32[4,512]{1,0:T(4,128)S(1)} %get-tuple-element.250, pred[512,2304]{1,0:T(8,128)(4,1)S(1)} %copy-done.2), kind=kLoop, calls=%fused_computation.15 | loop fusion | flops 18872320 | bytes 20070400 | tf_op jit(solution)/shard_map/reduce_sum | solution.py:64
  142.1 6.8 %fusion.29 = f32[512,4,64]{0,2,1:T(8,128)} fusion(bf16[2304,4,64]{0,2,1:T(8,128)(2,1)} %bitcast.197, f32[4,512,2304]{2,1,0:T(8,128)S(1)} %get-tuple-element.251, f32[4,512]{1,0:T(4,128)S(1)} %get-tuple-element.250, pred[512,2304]{1,0:T(8,128)(4,1)} %pad_add_fusion, f32[512,4]{0,1:T(4,128)} %get-tuple-element.228), kind=kOutput, calls=%fused_computation.38 | convolution fusion | flops 622985216 | bytes 21774336 | tf_op jit(solution)/shard_map/hbk,khd->bhd/dot_general | solution.py:65
  148.9 8.0 %fusion.26 = f32[512,4,64]{0,2,1:T(8,128)S(1)} fusion(f32[512,4,64]{0,2,1:T(8,128)} %fusion.29, bf16[2048,4,64]{0,2,1:T(8,128)(2,1)} %bitcast.198, f32[4,512,2048]{2,1,0:T(8,128)} %copy-done.1, f32[4,512]{1,0:T(4,128)S(1)} %copy-done.14, pred[512,2048]{1,0:T(8,128)(4,1)S(1)} %broadcast_and_fusion.1, f32[512,4]{0,1:T(4,128)S(1)} %get-tuple-element.227), kind=kOutput, calls=%fused_computation.37 | convolution fusion | flops 553910272 | bytes 19939328 | tf_op jit(solution)/shard_map/hbk,khd->bhd/dot_general | solution.py:65
  156.9 1.0 copy.83
  158.0 10.0 %fusion.79 = (bf16[32,128,1,256]{3,2,1,0:T(2,128)(2,1)}, bf16[32,128,1,256]{3,2,1,0:T(2,128)(2,1)}) fusion(bf16[32,128,2,256]{3,2,1,0:T(2,128)(2,1)} %param.30), kind=kLoop, calls=%fused_computation.141 | loop fusion | bytes 8388608 | tf_op jit(solution)/shard_map/slice | solution.py:85
  168.0 9.8 %copy.105 = bf16[32,128,1,256]{1,3,0,2:T(8,128)(2,1)} copy(bf16[32,128,1,256]{3,2,1,0:T(2,128)(2,1)} %get-tuple-element.229) | data formatting | bytes 4194304
  177.8 8.6 %copy.106 = bf16[32,128,1,256]{1,3,0,2:T(8,128)(2,1)S(1)} copy(bf16[32,128,1,256]{3,2,1,0:T(2,128)(2,1)} %get-tuple-element.230) | data formatting | bytes 4194304
  186.5 2.2 fusion.56
  189.0 1.2 fusion.54
  190.2 23.4 %all-gather = f32[8192,4]{0,1:T(4,128)S(1)} all-gather(f32[512,4]{0,1:T(4,128)S(1)} %get-tuple-element.245), channel_id=2, replica_groups=mesh['req'=16,'tp'=8] {'req'}, dimensions={0}, use_global_device_ids=true | all-gather | bytes 139264 | tf_op jit(solution)/shard_map/all_gather | solution.py:15
  213.6 21.6 %all-gather.1 = f32[8192,4]{0,1:T(4,128)S(1)} all-gather(f32[512,4]{0,1:T(4,128)S(1)} %get-tuple-element.226), channel_id=3, replica_groups=mesh['req'=16,'tp'=8] {'req'}, dimensions={0}, use_global_device_ids=true | all-gather | bytes 139264 | tf_op jit(solution)/shard_map/all_gather | solution.py:15
  235.2 1.1 slice_bitcast_fusion
  236.5 23.7 %while.19 = (s32[]{:T(128)}, f32[512,4]{0,1:T(4,128)S(1)}, f32[512,4]{0,1:T(4,128)S(1)}, f32[512,256]{0,1:T(8,128)S(1)}, f32[16,512,4]{1,2,0:T(4,128)S(1)}, /*in...) while((s32[]{:T(128)}, f32[512,4]{0,1:T(4,128)S(1)}, ...), condition=%wide.region_12.13_spmd, body=%wide.region_11.12_spmd.sunk | while | flops 405509 | bytes 3752087 | solution.py:21
  236.6 1.1 constant_dynamic-slice_fusion.3
  238.1 1.1 constant_dynamic-slice_fusion.3
  239.7 1.1 constant_dynamic-slice_fusion.3
  241.3 1.1 constant_dynamic-slice_fusion.3
  242.9 1.1 constant_dynamic-slice_fusion.3
  244.5 1.1 constant_dynamic-slice_fusion.3
  246.0 1.1 constant_dynamic-slice_fusion.3
  247.6 1.1 constant_dynamic-slice_fusion.3
  249.2 1.1 constant_dynamic-slice_fusion.3
  250.8 1.1 constant_dynamic-slice_fusion.3
  252.3 1.1 constant_dynamic-slice_fusion.3
  253.9 1.1 constant_dynamic-slice_fusion.3
  255.5 1.1 constant_dynamic-slice_fusion.3
  257.1 1.1 constant_dynamic-slice_fusion.3
  258.7 1.1 constant_dynamic-slice_fusion.3
  261.6 1.0 fusion.83
  262.7 10.1 %copy.110 = bf16[256,8,2,1024]{3,1,2,0:T(8,128)(2,1)} copy(bf16[256,8,2,1024]{3,2,1,0:T(2,128)(2,1)} %bitcast.182) | data formatting | bytes 16777216
  272.8 12.4 %copy.91 = bf16[2048,2048]{1,0:T(8,128)(2,1)} copy(bf16[2048,2048]{0,1:T(8,128)(2,1)} %bitcast.181) | data formatting | bytes 16777216 | tf_op jit(solution)/shard_map/dot_general | solution.py:231
  285.2 37.8 %all-reduce.2.cloned.1.call-done = f32[32,2048]{1,0:T(8,128)} async-done(((f32[32,2048]{1,0:T(8,128)}), f32[32,2048]{1,0:T(8,128)}) %all-reduce.2.cloned.1.call-update) | async-done | bytes 262160 | tf_op jit(solution)/shard_map/psum | solution.py:227
  323.0 1.1 multiply_reduce_fusion
  324.1 6.1 %fusion.40 = f32[32,2,1024]{2,0,1:T(8,128)S(1)} fusion(bf16[2,1024,2048]{2,1,0:T(8,128)(2,1)} %bitcast.180, f32[32,2048]{1,0:T(8,128)S(1)} %get-tuple-element.219, f32[2048]{0:T(1024)S(1)} %convert_element_type.94, f32[32]{0:T(128)S(1)} %add_rsqrt_fusion.1), kind=kOutput, calls=%fused_computation.56 | convolution fusion | flops 268632064 | bytes 8921216 | tf_op jit(solution)/shard_map/dot_general | solution.py:231
  330.2 1.5 fusion.48
  331.8 29.8 %reduce-scatter.2.cloned.1.call-done = f32[32,256]{1,0:T(8,128)} async-done(((f32[32,2048]{1,0:T(8,128)}), f32[32,256]{1,0:T(8,128)}) %reduce-scatter.2.cloned.1.call-update) | async-done | bytes 32784 | tf_op jit(solution)/shard_map/reduce_scatter | solution.py:235
  361.6 1.4 add_convert_fusion.2
  (152 shorter events, 22.0 us)
Async XLA Ops:
  6.5 255.1 %copy-start = (bf16[256,2048]{1,0:T(8,128)(2,1)S(1)}, bf16[256,2048]{1,0:T(8,128)(2,1)}, u32[]{:S(2)}) copy-start(bf16[256,2048]{1,0:T(8,128)(2,1)} %param.25) | copy-start | bytes 3145732
  6.5 89.2 %all-gather.5.cloned.1.call-start = ((), (), s32[]{:S(2)}) async-start(), calls=%async_computation.1 | async-start | bytes 1179648 | tf_op jit(solution)/shard_map/all_gather | solution.py:150
  7.3 228.0 %all-gather.7.cloned.1.call-start = ((), (), s32[]{:S(2)}) async-start(), calls=%async_computation.2 | async-start | bytes 8912896 | tf_op jit(solution)/shard_map/all_gather | solution.py:15
  16.6 4.6 %copy-start.7 = (bf16[32,2048]{1,0:T(8,128)(2,1)S(1)}, bf16[32,2048]{1,0:T(8,128)(2,1)}, u32[]{:S(2)}) copy-start(bf16[32,2048]{1,0:T(8,128)(2,1)} %param.20) | copy-start | bytes 393220
  18.7 5.4 %copy-start.21 = (s32[8]{0:T(128)S(1)}, s32[8]{0:T(128)}, u32[]{:S(2)}) copy-start(s32[8]{0:T(128)} %param.33) | copy-start | bytes 100
  18.7 5.5 %copy-start.19 = (s32[32]{0:T(128)S(1)}, s32[32]{0:T(128)}, u32[]{:S(2)}) copy-start(s32[32]{0:T(128)} %param.35) | copy-start | bytes 388
  21.2 33.4 %copy-start.3 = (bf16[8,256,2,256]{3,2,1,0:T(2,128)(2,1)S(1)}, bf16[8,256,2,256]{3,2,1,0:T(2,128)(2,1)}, u32[]{:S(2)}) copy-start(bf16[8,256,2,256]{3,2,1,0:T(2,128)(2,1)} %param.28) | copy-start | bytes 6291460
  24.1 0.7 copy-start.9
  25.5 0.6 copy-start.11
  54.6 11.5 %copy-start.18 = (s32[1,256]{1,0:T(1,128)S(1)}, s32[1,256]{1,0:T(1,128)}, u32[]{:S(2)}) copy-start(s32[1,256]{1,0:T(1,128)} %param.32) | copy-start | bytes 3076
  58.8 12.8 %copy-start.4 = (bf16[2048,1,256]{2,1,0:T(2,128)(2,1)S(1)}, bf16[2048,1,256]{2,1,0:T(2,128)(2,1)}, u32[]{:S(2)}) copy-start(bf16[2048,1,256]{2,1,0:T(2,128)(2,1)} %get-tuple-element.233) | copy-start | bytes 3145732
  75.9 4.5 %copy-start.5 = (bf16[2048,1,256]{0,2,1:T(8,128)(2,1)S(1)}, bf16[2048,1,256]{0,2,1:T(8,128)(2,1)}, u32[]{:S(2)}) copy-start(bf16[2048,1,256]{0,2,1:T(8,128)(2,1)} %copy.103) | copy-start | bytes 3145732
  84.9 5.7 %copy-start.1 = (f32[4,512,2048]{2,1,0:T(8,128)}, f32[4,512,2048]{2,1,0:T(8,128)S(1)}, u32[]{:S(2)}) copy-start(f32[4,512,2048]{2,1,0:T(8,128)S(1)} %get-tuple-element.253) | copy-start | bytes 50331652
  84.9 5.7 %copy-start.13 = (f32[4,512]{1,0:T(4,128)}, f32[4,512]{1,0:T(4,128)S(1)}, u32[]{:S(2)}) copy-start(f32[4,512]{1,0:T(4,128)S(1)} %get-tuple-element.252) | copy-start | bytes 24580
  95.8 4.3 %copy-start.10 = (f32[256,32]{0,1:T(8,128)S(1)}, f32[256,32]{0,1:T(8,128)}, u32[]{:S(2)}) copy-start(f32[256,32]{0,1:T(8,128)} %get-tuple-element.247) | copy-start | bytes 98308
  130.7 5.6 %copy-start.2 = (pred[512,2304]{1,0:T(8,128)(4,1)S(1)}, pred[512,2304]{1,0:T(8,128)(4,1)}, u32[]{:S(2)}) copy-start(pred[512,2304]{1,0:T(8,128)(4,1)} %pad_add_fusion) | copy-start | bytes 3538948
  136.4 5.1 %copy-start.14 = (f32[4,512]{1,0:T(4,128)S(1)}, f32[4,512]{1,0:T(4,128)}, u32[]{:S(2)}) copy-start(f32[4,512]{1,0:T(4,128)} %copy-done.13) | copy-start | bytes 24580
  136.4 5.1 %copy-start.15 = (f32[4,512]{1,0:T(4,128)S(1)}, f32[4,512]{1,0:T(4,128)}, u32[]{:S(2)}) copy-start(f32[4,512]{1,0:T(4,128)} %fusion.6) | copy-start | bytes 24580
  157.9 165.1 %all-reduce.2.cloned.1.call-start = ((), (), s32[]{:S(2)}) async-start(), calls=%async_computation.3 | async-start | bytes 524288 | tf_op jit(solution)/shard_map/psum | solution.py:227
  177.8 8.6 %copy-start.20 = (s32[32]{0:T(128)S(1)}, s32[32]{0:T(128)}, u32[]{:S(2)}) copy-start(s32[32]{0:T(128)} %param.35) | copy-start | bytes 388
  177.8 8.7 %copy-start.12 = (bf16[32,4,64]{2,0,1:T(8,128)(2,1)S(1)}, bf16[32,4,64]{2,0,1:T(8,128)(2,1)}, u32[]{:S(2)}) copy-start(bf16[32,4,64]{2,0,1:T(8,128)(2,1)} %copy-done.11) | copy-start | bytes 49156
  236.5 23.9 %copy-start.16 = (f32[32,4]{0,1:T(4,128)S(1)}, f32[32,4]{0,1:T(4,128)}, u32[]{:S(2)}) copy-start(f32[32,4]{0,1:T(4,128)} %get-tuple-element.224) | copy-start | bytes 1540
  262.6 99.0 %reduce-scatter.2.cloned.1.call-start = ((), (), s32[]{:S(2)}) async-start(), calls=%async_computation.4 | async-start | bytes 294912 | tf_op jit(solution)/shard_map/reduce_scatter | solution.py:235
  272.8 12.4 %copy-start.17 = (bf16[2048]{0:T(1024)(128)(2,1)S(1)}, bf16[2048]{0:T(1024)(128)(2,1)}, u32[]{:S(2)}) copy-start(bf16[2048]{0:T(1024)(128)(2,1)} %param.22) | copy-start | bytes 12292
  272.8 50.2 %copy-start.8 = (bf16[32,2048]{1,0:T(8,128)(2,1)S(1)}, bf16[32,2048]{1,0:T(8,128)(2,1)}, u32[]{:S(2)}) copy-start(bf16[32,2048]{1,0:T(8,128)(2,1)} %param.20) | copy-start | bytes 393220
  324.1 6.2 %copy-start.6 = (bf16[1024,2048]{1,0:T(8,128)(2,1)S(1)}, bf16[1024,2048]{1,0:T(8,128)(2,1)}, u32[]{:S(2)}) copy-start(bf16[1024,2048]{1,0:T(8,128)(2,1)} %param.27) | copy-start | bytes 12582916
Sparse Core Ops, SparseCore 0:
  9.0 26.0 all-gather.4
  158.0 71.9 all-gather.6
  262.7 60.1 all-reduce.1
  331.9 29.6 reduce-scatter.1
where the time goes:
time: 372 us; the launch traced here: 370 us
  local copies, waits for them, and re-layouts  124 us (33%)
  blocking collectives  69.1 us (19%)
  waiting for transfers between devices  68.4 us (18%)
  other arithmetic  50 us (13%)
  matrix products  44.2 us (12%)
  between operations  13.5 us (4%)
    unnamed x53, local copies, waits for them, and re-layouts  49.1 us
    all_gather x2, blocking collectives, combined_all(): everything = jax.tree.map(lambda part: lax.all_gather(part, axis), value)  45 us
    psum x1, waiting for transfers between devices, on_device(): residual = stream_float + lax.psum(attn_part, 'tp')  37.8 us
    reduce_scatter x1, waiting for transfers between devices, on_device(): lax.psum_scatter(jnp.dot(hidden, w_down, preferred_element_type=jnp.float...  29.8 us
    all_gather x1, blocking collectives, on_device(): lax.all_gather(queries.reshape(own_rows, query_width), 'req', axis=0, til...  24.1 us
    dynamic_slice x30, local copies, waits for them, and re-layouts, lap(): return combine(so_far, jax.tree.map(lambda part: part[k], everything))  19.2 us
    slice x3, local copies, waits for them, and re-layouts, partial_softmax(): value_part = key_rows[:, 1].reshape(count, heads, HEAD_DIM)  15 us
    dot_general x2, matrix products, partial_softmax(): jnp.einsum('hbk,khd->bhd', weights.astype(jnp.bfloat16), value_part, pref...  14.8 us
  transfers between devices with their start and end apart: 4, of which 2 were waited for; matrix products, arithmetic and copies ran while one was open for 30% of the time, Pallas kernels for 0%

commit v1 on v0

--- a/solution.py
+++ b/solution.py
@@ -224,7 +224,7 @@
     attn_part = jnp.dot(attended, w_out, preferred_element_type=jnp.float32)
     width_share = D // lax.axis_size("tp")
     tp_rank = lax.axis_index("tp")
-    residual = stream_float + lax.psum(attn_part, "tp")
+    residual = stream_float + jnp.sum(lax.all_gather(attn_part, "tp"), axis=0)
     mixed_in = rms_scale(residual, mlp_gain).astype(jnp.bfloat16)
     residual_share = lax.dynamic_slice_in_dim(residual, tp_rank * width_share, width_share, 1)
     hidden_width = w_gate_up.shape[2]

time: 372 us -> 340 us (0.914)
  waiting for transfers between devices: 68.4 us -> 35.1 us
    psum x1 -> x0, waiting for transfers between devices: 37.8 us -> none  [on_device(): residual = stream_float + lax.psum(attn_part, 'tp')]
  transfers between devices with their start and end apart: 4 -> 4, of which waited for: 2 -> 2; matrix products, arithmetic and copies ran while one was open for 30% -> 33% of each run, Pallas kernels for 0% -> 0%
where the time goes in v1:
time: 340 us; the launch traced here: 337 us
  local copies, waits for them, and re-layouts  124 us (36%)
  blocking collectives  69.1 us (20%)
  other arithmetic  50.8 us (15%)
  matrix products  44.2 us (13%)
  waiting for transfers between devices  35.1 us (10%)
  between operations  13.6 us (4%)
    unnamed x53, local copies, waits for them, and re-layouts  49.1 us
    all_gather x2, blocking collectives, combined_all(): everything = jax.tree.map(lambda part: lax.all_gather(part, axis), value)  45 us
    reduce_scatter x1, waiting for transfers between devices, on_device(): lax.psum_scatter(jnp.dot(hidden, w_down, preferred_element_type=jnp.float...  31.3 us
    all_gather x1, blocking collectives, on_device(): lax.all_gather(queries.reshape(own_rows, query_width), 'req', axis=0, til...  24.1 us
    dynamic_slice x30, local copies, waits for them, and re-layouts, lap(): return combine(so_far, jax.tree.map(lambda part: part[k], everything))  19.2 us
    slice x3, local copies, waits for them, and re-layouts, partial_softmax(): value_part = key_rows[:, 1].reshape(count, heads, HEAD_DIM)  15 us
    dot_general x2, matrix products, partial_softmax(): jnp.einsum('hbk,khd->bhd', weights.astype(jnp.bfloat16), value_part, pref...  14.8 us
    concatenate x1, other arithmetic, on_device(): jnp.concatenate([mid_cache.reshape(node_count * slots, 2, query_width), r...  13.3 us
  transfers between devices with their start and end apart: 4, of which 2 were waited for; matrix products, arithmetic and copies ran while one was open for 33% of the time, Pallas kernels for 0%

profile of v1, /device:TPU:0, one launch (start us, length us, event | category | flops | bytes accessed | tf_op | source)
XLA Modules:
  0.0 337.1 jit_solution(5786178928298028482)
XLA Ops:
  9.8 1.3 dynamic_slice.57
  11.1 1.2 dynamic_slice.56
  13.7 1.0 fusion.36
  14.8 1.6 fusion.62
  16.6 2.1 copy.109
  18.7 2.5 copy.77
  21.2 2.8 fusion.44
  26.2 24.1 %all_gather.28 = bf16[512,256]{1,0:T(8,128)(2,1)S(1)} all-gather(bf16[32,256]{1,0:T(8,128)(2,1)S(1)} %convert_element_type.81), channel_id=1, replica_groups=mesh['req'=16,'tp'=8] {'req'}, dimensions={0}, use_global_device_ids=true | all-gather | bytes 278528 | tf_op jit(solution)/shard_map/all_gather | solution.py:166
  51.2 1.8 and.64
  53.0 1.6 copy.107
  54.6 4.2 %fusion.81 = (bf16[2048,1,256]{2,1,0:T(2,128)(2,1)}, bf16[2048,1,256]{2,1,0:T(2,128)(2,1)}) fusion(bf16[2048,2,256]{2,1,0:T(2,128)(2,1)S(1)} %bitcast.184), kind=kLoop, calls=%fused_computation.143 | loop fusion | bytes 4194304 | tf_op jit(solution)/shard_map/slice | solution.py:56
  58.8 6.0 %copy.103 = bf16[2048,1,256]{0,2,1:T(8,128)(2,1)} copy(bf16[2048,1,256]{2,1,0:T(2,128)(2,1)} %get-tuple-element.234) | data formatting | bytes 2097152
  64.8 1.3 fusion.70
  69.3 1.5 broadcast_and_fusion
  71.6 4.3 %copy.104 = bf16[2048,1,256]{0,2,1:T(8,128)(2,1)} copy(bf16[2048,1,256]{2,1,0:T(2,128)(2,1)S(1)} %copy-done.4) | data formatting | bytes 2097152
  75.9 1.9 broadcast_and_fusion.1
  77.9 2.5 pad_add_fusion
  80.3 4.5 %select_reduce_fusion.1 = (f32[4,512]{1,0:T(4,128)S(1)}, f32[4,512,2048]{2,1,0:T(8,128)S(1)}) fusion(pred[512,2048]{1,0:T(8,128)(4,1)S(1)} %broadcast_and_fusion.1, bf16[512,4,64]{0,2,1:T(8,128)(2,1)} %bitcast.190, bf16[2048,4,64]{0,2,1:T(8,128)(2,1)S(1)} %bitcast.189), kind=kOutput, calls=%fused_computation.13 | convolution fusion | flops 549451776 | bytes 19144704 | tf_op jit(solution)/shard_map/bhd,khd->hbk/dot_general | solution.py:58
  84.9 5.7 %copy-done.1 = f32[4,512,2048]{2,1,0:T(8,128)} copy-done((f32[4,512,2048]{2,1,0:T(8,128)}, f32[4,512,2048]{2,1,0:T(8,128)S(1)}, u32[]{:S(2)}) %copy-start.1) | copy-done | bytes 16777240
  90.6 5.2 %fusion.6 = f32[4,512]{1,0:T(4,128)} fusion(f32[4,512,2048]{2,1,0:T(8,128)S(1)} %get-tuple-element.253, f32[4,512]{1,0:T(4,128)S(1)} %get-tuple-element.252, pred[512,2048]{1,0:T(8,128)(4,1)S(1)} %broadcast_and_fusion.1), kind=kLoop, calls=%fused_computation.17 | loop fusion | flops 16775168 | bytes 17842176 | tf_op jit(solution)/shard_map/reduce_sum | solution.py:64
  95.8 1.5 fusion.13
  97.3 2.8 convolution_bitcast_fusion
  100.6 13.3 %maximum_maximum_fusion = bf16[2304,2,256]{2,1,0:T(2,128)(2,1)S(1)} fusion(bf16[256,1,256]{2,1,0:T(2,128)(2,1)S(1)} %copy.79, bf16[256,1,256]{2,1,0:T(2,128)(2,1)S(1)} %copy.78, bf16[2048,2,256]{2,1,0:T(2,128)(2,1)} %bitcast.198), kind=kLoop, calls=%fused_computation.25 | loop fusion | flops 7077888 | bytes 4718592 | tf_op jit(solution)/shard_map/concatenate | solution.py:193
  113.9 4.8 %fusion.80 = (bf16[2304,1,256]{2,1,0:T(2,128)(2,1)}, bf16[2304,1,256]{2,1,0:T(2,128)(2,1)}) fusion(bf16[2304,2,256]{2,1,0:T(2,128)(2,1)S(1)} %maximum_maximum_fusion), kind=kLoop, calls=%fused_computation.142 | loop fusion | bytes 4718592 | tf_op jit(solution)/shard_map/slice | solution.py:56
  118.7 6.0 %copy.80 = bf16[2304,1,256]{0,2,1:T(8,128)(2,1)} copy(bf16[2304,1,256]{2,1,0:T(2,128)(2,1)} %get-tuple-element.232) | data formatting | bytes 2359296 | tf_op jit(solution)/shard_map/slice | solution.py:55
  124.7 6.0 %copy.82 = bf16[2304,1,256]{0,2,1:T(8,128)(2,1)} copy(bf16[2304,1,256]{2,1,0:T(2,128)(2,1)} %get-tuple-element.231) | data formatting | bytes 2359296 | tf_op jit(solution)/shard_map/slice | solution.py:56
  130.7 5.6 %select_reduce_fusion = (f32[4,512]{1,0:T(4,128)S(1)}, f32[4,512,2304]{2,1,0:T(8,128)S(1)}) fusion(pred[512,2304]{1,0:T(8,128)(4,1)} %pad_add_fusion, bf16[512,4,64]{0,2,1:T(8,128)(2,1)} %bitcast.191, bf16[2304,4,64]{0,2,1:T(8,128)(2,1)} %bitcast.188), kind=kOutput, calls=%fused_computation.11 | convolution fusion | flops 618133504 | bytes 21504000 | tf_op jit(solution)/shard_map/bhd,khd->hbk/dot_general | solution.py:58
  136.4 5.1 %fusion.4 = f32[4,512]{1,0:T(4,128)S(1)} fusion(f32[4,512,2304]{2,1,0:T(8,128)S(1)} %get-tuple-element.251, f32[4,512]{1,0:T(4,128)S(1)} %get-tuple-element.250, pred[512,2304]{1,0:T(8,128)(4,1)S(1)} %copy-done.2), kind=kLoop, calls=%fused_computation.15 | loop fusion | flops 18872320 | bytes 20070400 | tf_op jit(solution)/shard_map/reduce_sum | solution.py:64
  142.1 6.8 %fusion.29 = f32[512,4,64]{0,2,1:T(8,128)} fusion(bf16[2304,4,64]{0,2,1:T(8,128)(2,1)} %bitcast.199, f32[4,512,2304]{2,1,0:T(8,128)S(1)} %get-tuple-element.251, f32[4,512]{1,0:T(4,128)S(1)} %get-tuple-element.250, pred[512,2304]{1,0:T(8,128)(4,1)} %pad_add_fusion, f32[512,4]{0,1:T(4,128)} %get-tuple-element.228), kind=kOutput, calls=%fused_computation.38 | convolution fusion | flops 622985216 | bytes 21774336 | tf_op jit(solution)/shard_map/hbk,khd->bhd/dot_general | solution.py:65
  148.9 8.0 %fusion.26 = f32[512,4,64]{0,2,1:T(8,128)S(1)} fusion(f32[512,4,64]{0,2,1:T(8,128)} %fusion.29, bf16[2048,4,64]{0,2,1:T(8,128)(2,1)} %bitcast.200, f32[4,512,2048]{2,1,0:T(8,128)} %copy-done.1, f32[4,512]{1,0:T(4,128)S(1)} %copy-done.14, pred[512,2048]{1,0:T(8,128)(4,1)S(1)} %broadcast_and_fusion.1, f32[512,4]{0,1:T(4,128)S(1)} %get-tuple-element.227), kind=kOutput, calls=%fused_computation.37 | convolution fusion | flops 553910272 | bytes 19939328 | tf_op jit(solution)/shard_map/hbk,khd->bhd/dot_general | solution.py:65
  156.9 1.0 copy.83
  158.0 10.0 %fusion.79 = (bf16[32,128,1,256]{3,2,1,0:T(2,128)(2,1)}, bf16[32,128,1,256]{3,2,1,0:T(2,128)(2,1)}) fusion(bf16[32,128,2,256]{3,2,1,0:T(2,128)(2,1)} %param.30), kind=kLoop, calls=%fused_computation.141 | loop fusion | bytes 8388608 | tf_op jit(solution)/shard_map/slice | solution.py:85
  168.0 9.8 %copy.105 = bf16[32,128,1,256]{1,3,0,2:T(8,128)(2,1)} copy(bf16[32,128,1,256]{3,2,1,0:T(2,128)(2,1)} %get-tuple-element.229) | data formatting | bytes 4194304
  177.8 8.6 %copy.106 = bf16[32,128,1,256]{1,3,0,2:T(8,128)(2,1)S(1)} copy(bf16[32,128,1,256]{3,2,1,0:T(2,128)(2,1)} %get-tuple-element.230) | data formatting | bytes 4194304
  186.5 2.2 fusion.56
  189.0 1.2 fusion.54
  190.2 23.4 %all-gather = f32[8192,4]{0,1:T(4,128)S(1)} all-gather(f32[512,4]{0,1:T(4,128)S(1)} %get-tuple-element.245), channel_id=2, replica_groups=mesh['req'=16,'tp'=8] {'req'}, dimensions={0}, use_global_device_ids=true | all-gather | bytes 139264 | tf_op jit(solution)/shard_map/all_gather | solution.py:15
  213.6 21.6 %all-gather.1 = f32[8192,4]{0,1:T(4,128)S(1)} all-gather(f32[512,4]{0,1:T(4,128)S(1)} %get-tuple-element.226), channel_id=3, replica_groups=mesh['req'=16,'tp'=8] {'req'}, dimensions={0}, use_global_device_ids=true | all-gather | bytes 139264 | tf_op jit(solution)/shard_map/all_gather | solution.py:15
  235.2 1.1 slice_bitcast_fusion
  236.5 23.7 %while.19 = (s32[]{:T(128)}, f32[512,4]{0,1:T(4,128)S(1)}, f32[512,4]{0,1:T(4,128)S(1)}, f32[512,256]{0,1:T(8,128)S(1)}, f32[16,512,4]{1,2,0:T(4,128)S(1)}, /*in...) while((s32[]{:T(128)}, f32[512,4]{0,1:T(4,128)S(1)}, ...), condition=%wide.region_12.13_spmd, body=%wide.region_11.12_spmd.sunk | while | flops 405509 | bytes 3752087 | solution.py:21
  236.6 1.1 constant_dynamic-slice_fusion.3
  238.1 1.1 constant_dynamic-slice_fusion.3
  239.7 1.1 constant_dynamic-slice_fusion.3
  241.3 1.1 constant_dynamic-slice_fusion.3
  242.9 1.1 constant_dynamic-slice_fusion.3
  244.5 1.1 constant_dynamic-slice_fusion.3
  246.0 1.1 constant_dynamic-slice_fusion.3
  247.6 1.1 constant_dynamic-slice_fusion.3
  249.2 1.1 constant_dynamic-slice_fusion.3
  250.8 1.1 constant_dynamic-slice_fusion.3
  252.4 1.1 constant_dynamic-slice_fusion.3
  253.9 1.1 constant_dynamic-slice_fusion.3
  255.5 1.1 constant_dynamic-slice_fusion.3
  257.1 1.1 constant_dynamic-slice_fusion.3
  258.7 1.1 constant_dynamic-slice_fusion.3
  261.6 1.0 fusion.83
  262.7 10.1 %copy.110 = bf16[256,8,2,1024]{3,1,2,0:T(8,128)(2,1)} copy(bf16[256,8,2,1024]{3,2,1,0:T(2,128)(2,1)} %bitcast.183) | data formatting | bytes 16777216
  272.8 12.5 %copy.91 = bf16[2048,2048]{1,0:T(8,128)(2,1)} copy(bf16[2048,2048]{0,1:T(8,128)(2,1)} %bitcast.182) | data formatting | bytes 16777216 | tf_op jit(solution)/shard_map/dot_general | solution.py:231
  285.3 3.0 all-gather.11.cloned.1.call-done
  288.3 1.7 reduce_sum.126
  290.2 6.1 %fusion.40 = f32[32,2,1024]{2,0,1:T(8,128)S(1)} fusion(bf16[2,1024,2048]{2,1,0:T(8,128)(2,1)} %bitcast.181, f32[32,2048]{1,0:T(8,128)S(1)} %get-tuple-element.219, f32[2048]{0:T(1024)S(1)} %convert_element_type.94, f32[32]{0:T(128)S(1)} %add_rsqrt_fusion.1), kind=kOutput, calls=%fused_computation.56 | convolution fusion | flops 268632064 | bytes 8921216 | tf_op jit(solution)/shard_map/dot_general | solution.py:231
  296.4 1.5 fusion.48
  297.9 31.3 %reduce-scatter.2.cloned.1.call-done = f32[32,256]{1,0:T(8,128)} async-done(((f32[32,2048]{1,0:T(8,128)}), f32[32,256]{1,0:T(8,128)}) %reduce-scatter.2.cloned.1.call-update) | async-done | bytes 32784 | tf_op jit(solution)/shard_map/reduce_scatter | solution.py:235
  329.2 1.4 add_convert_fusion.2
  (153 shorter events, 22.2 us)
Async XLA Ops:
  6.5 255.1 %copy-start = (bf16[256,2048]{1,0:T(8,128)(2,1)S(1)}, bf16[256,2048]{1,0:T(8,128)(2,1)}, u32[]{:S(2)}) copy-start(bf16[256,2048]{1,0:T(8,128)(2,1)} %param.25) | copy-start | bytes 3145732
  6.5 89.2 %all-gather.7.cloned.1.call-start = ((), (), s32[]{:S(2)}) async-start(), calls=%async_computation.1 | async-start | bytes 1179648 | tf_op jit(solution)/shard_map/all_gather | solution.py:150
  7.3 228.0 %all-gather.9.cloned.1.call-start = ((), (), s32[]{:S(2)}) async-start(), calls=%async_computation.2 | async-start | bytes 8912896 | tf_op jit(solution)/shard_map/all_gather | solution.py:15
  16.6 4.6 %copy-start.7 = (bf16[32,2048]{1,0:T(8,128)(2,1)S(1)}, bf16[32,2048]{1,0:T(8,128)(2,1)}, u32[]{:S(2)}) copy-start(bf16[32,2048]{1,0:T(8,128)(2,1)} %param.20) | copy-start | bytes 393220
  18.7 5.4 %copy-start.21 = (s32[8]{0:T(128)S(1)}, s32[8]{0:T(128)}, u32[]{:S(2)}) copy-start(s32[8]{0:T(128)} %param.33) | copy-start | bytes 100
  18.7 5.5 %copy-start.19 = (s32[32]{0:T(128)S(1)}, s32[32]{0:T(128)}, u32[]{:S(2)}) copy-start(s32[32]{0:T(128)} %param.35) | copy-start | bytes 388
  21.2 33.4 %copy-start.3 = (bf16[8,256,2,256]{3,2,1,0:T(2,128)(2,1)S(1)}, bf16[8,256,2,256]{3,2,1,0:T(2,128)(2,1)}, u32[]{:S(2)}) copy-start(bf16[8,256,2,256]{3,2,1,0:T(2,128)(2,1)} %param.28) | copy-start | bytes 6291460
  24.1 0.7 copy-start.9
  25.5 0.6 copy-start.11
  54.6 11.5 %copy-start.18 = (s32[1,256]{1,0:T(1,128)S(1)}, s32[1,256]{1,0:T(1,128)}, u32[]{:S(2)}) copy-start(s32[1,256]{1,0:T(1,128)} %param.32) | copy-start | bytes 3076
  58.8 12.8 %copy-start.4 = (bf16[2048,1,256]{2,1,0:T(2,128)(2,1)S(1)}, bf16[2048,1,256]{2,1,0:T(2,128)(2,1)}, u32[]{:S(2)}) copy-start(bf16[2048,1,256]{2,1,0:T(2,128)(2,1)} %get-tuple-element.233) | copy-start | bytes 3145732
  75.9 4.5 %copy-start.5 = (bf16[2048,1,256]{0,2,1:T(8,128)(2,1)S(1)}, bf16[2048,1,256]{0,2,1:T(8,128)(2,1)}, u32[]{:S(2)}) copy-start(bf16[2048,1,256]{0,2,1:T(8,128)(2,1)} %copy.103) | copy-start | bytes 3145732
  84.9 5.7 %copy-start.1 = (f32[4,512,2048]{2,1,0:T(8,128)}, f32[4,512,2048]{2,1,0:T(8,128)S(1)}, u32[]{:S(2)}) copy-start(f32[4,512,2048]{2,1,0:T(8,128)S(1)} %get-tuple-element.253) | copy-start | bytes 50331652
  84.9 5.7 %copy-start.13 = (f32[4,512]{1,0:T(4,128)}, f32[4,512]{1,0:T(4,128)S(1)}, u32[]{:S(2)}) copy-start(f32[4,512]{1,0:T(4,128)S(1)} %get-tuple-element.252) | copy-start | bytes 24580
  95.8 4.3 %copy-start.10 = (f32[256,32]{0,1:T(8,128)S(1)}, f32[256,32]{0,1:T(8,128)}, u32[]{:S(2)}) copy-start(f32[256,32]{0,1:T(8,128)} %get-tuple-element.247) | copy-start | bytes 98308
  130.7 5.6 %copy-start.2 = (pred[512,2304]{1,0:T(8,128)(4,1)S(1)}, pred[512,2304]{1,0:T(8,128)(4,1)}, u32[]{:S(2)}) copy-start(pred[512,2304]{1,0:T(8,128)(4,1)} %pad_add_fusion) | copy-start | bytes 3538948
  136.4 5.1 %copy-start.14 = (f32[4,512]{1,0:T(4,128)S(1)}, f32[4,512]{1,0:T(4,128)}, u32[]{:S(2)}) copy-start(f32[4,512]{1,0:T(4,128)} %copy-done.13) | copy-start | bytes 24580
  136.4 5.1 %copy-start.15 = (f32[4,512]{1,0:T(4,128)S(1)}, f32[4,512]{1,0:T(4,128)}, u32[]{:S(2)}) copy-start(f32[4,512]{1,0:T(4,128)} %fusion.6) | copy-start | bytes 24580
  157.9 130.4 %all-gather.11.cloned.1.call-start = ((), (), s32[]{:S(2)}) async-start(), calls=%async_computation.4 | async-start | bytes 2359296 | tf_op jit(solution)/shard_map/all_gather | solution.py:227
  177.8 8.6 %copy-start.20 = (s32[32]{0:T(128)S(1)}, s32[32]{0:T(128)}, u32[]{:S(2)}) copy-start(s32[32]{0:T(128)} %param.35) | copy-start | bytes 388
  177.8 8.7 %copy-start.12 = (bf16[32,4,64]{2,0,1:T(8,128)(2,1)S(1)}, bf16[32,4,64]{2,0,1:T(8,128)(2,1)}, u32[]{:S(2)}) copy-start(bf16[32,4,64]{2,0,1:T(8,128)(2,1)} %copy-done.11) | copy-start | bytes 49156
  236.5 23.9 %copy-start.16 = (f32[32,4]{0,1:T(4,128)S(1)}, f32[32,4]{0,1:T(4,128)}, u32[]{:S(2)}) copy-start(f32[32,4]{0,1:T(4,128)} %get-tuple-element.224) | copy-start | bytes 1540
  262.7 66.5 %reduce-scatter.2.cloned.1.call-start = ((), (), s32[]{:S(2)}) async-start(), calls=%async_computation.3 | async-start | bytes 294912 | tf_op jit(solution)/shard_map/reduce_scatter | solution.py:235
  272.8 12.5 %copy-start.17 = (bf16[2048]{0:T(1024)(128)(2,1)S(1)}, bf16[2048]{0:T(1024)(128)(2,1)}, u32[]{:S(2)}) copy-start(bf16[2048]{0:T(1024)(128)(2,1)} %param.22) | copy-start | bytes 12292
  272.8 17.2 %copy-start.8 = (bf16[32,2048]{1,0:T(8,128)(2,1)S(1)}, bf16[32,2048]{1,0:T(8,128)(2,1)}, u32[]{:S(2)}) copy-start(bf16[32,2048]{1,0:T(8,128)(2,1)} %param.20) | copy-start | bytes 393220
  290.2 6.1 %copy-start.6 = (bf16[1024,2048]{1,0:T(8,128)(2,1)S(1)}, bf16[1024,2048]{1,0:T(8,128)(2,1)}, u32[]{:S(2)}) copy-start(bf16[1024,2048]{1,0:T(8,128)(2,1)} %param.27) | copy-start | bytes 12582916
Sparse Core Ops, SparseCore 0:
  9.0 26.0 all-gather.6
  158.0 71.9 all-gather.8
  262.8 25.5 all-gather.10
  298.0 31.0 reduce-scatter.1
